TPU v7x, 32 devices: a whole 2x2x4 slice. The times are simulated.
32 devices in a mesh: vx: 2 (over x), vy: 4 (over y, core), scan: 4 (over z).
Axes of the slice: x: 2, y: 2, z: 4, core: 2. Of those that a mesh axis runs over, the one named last changes fastest.
Arguments:
- volume: bfloat16 [2, 64, 256, 256], P(None, 'vx', 'vy'), may hold values from -6 to 6
- tile_matrix: bfloat16 [4, 2, 8, 1024, 128], P('scan', 'vx', 'vy'), may hold values from -0.09375 to 0.09375
- tile_offset: int32 [4, 2, 8], P('scan', 'vx', 'vy'), may hold values from 0 to 384
- patch_count: int32 [4, 8], P('scan', ('vx', 'vy')), may hold values from 1 to 3, as said below
- scan_position: int32 [4, 8, 3, 2], P('scan', ('vx', 'vy')), may hold values from 0 to 256, as said below
- measured: float32 [4, 8, 3, 256, 256], P('scan', ('vx', 'vy')), may hold values from 0.2 to 5
- illumination: float32 [2, 256, 256], replicated, may hold values from -6 to 6
Outputs:
- change: float32 [2, 64, 256, 256], P(None, 'vx', 'vy', 'scan')
Inputs may be any that keep to these rules, and one draw needn't show every extreme that they name: `patch_count`: an owner's slots below its count hold measured patches, the others are unused; at every angle some owner holds 3. `scan_position`: column 0 is a patch's first detector column, 0 to 256; column 1 its first row, 0 to 0.
All inputs are finite; a program needn't handle non-finite values.
Results may differ from a plain program's by a relative error of at most 0.0085.
Values may be sent and summed in bfloat16 or wider, within the bound.
No kernel may reach another device: no remote copies, remote signals or barrier semaphores. Data moves between devices by JAX's collectives and lax.ppermute only.
A program may use at most 64 MiB of HBM per device.

v0:
```python
import math
import jax
import jax.numpy as jnp
from jax import lax
from jax.sharding import PartitionSpec as P

TILE = 32
NZ = 256
U = 512
TU = 128
PATCH_SIDE = 256
ABSORPTION = 0.2
STEP_LENGTH = 0.003


def dft_tables(length):
    counter = jnp.arange(length, dtype=jnp.int32)
    product = counter[:, None] * counter[None, :] % length
    radians = product.astype(jnp.float32) * (2.0 * math.pi / length)
    scaling = 1.0 / math.sqrt(length)
    return (jnp.cos(radians) * scaling, jnp.sin(radians) * scaling)


def matmul(left, right):
    return jnp.dot(left, right, precision=lax.Precision.HIGHEST)


def patch_misfit(window, illumination, intensity, cosine_table, sine_table):
    amplitude = jnp.exp(-ABSORPTION * window[1])
    trans_re = amplitude * jnp.cos(window[0])
    trans_im = amplitude * jnp.sin(window[0])
    exit_re = illumination[0] * trans_re - illumination[1] * trans_im
    exit_im = illumination[0] * trans_im + illumination[1] * trans_re
    half_re = matmul(cosine_table, exit_re) + matmul(sine_table, exit_im)
    half_im = matmul(cosine_table, exit_im) - matmul(sine_table, exit_re)
    far_re = matmul(half_re, cosine_table) + matmul(half_im, sine_table)
    far_im = matmul(half_im, cosine_table) - matmul(half_re, sine_table)
    residue = far_re * far_re + far_im * far_im - intensity
    return jnp.sum(residue * residue)


def place_patch(summed_total, slope, corner):
    anchor = (jnp.zeros((), jnp.int32), corner[0], corner[1])
    before = lax.dynamic_slice(summed_total, anchor, slope.shape)
    return lax.dynamic_update_slice(summed_total, before + slope, anchor)


def patch_term(
    summed_total, projected_field, corner, intensity, illumination, cosine_table, sine_table
):
    anchor = (jnp.zeros((), jnp.int32), corner[0], corner[1])
    window = lax.dynamic_slice(projected_field, anchor, (2, PATCH_SIDE, PATCH_SIDE))
    slope = jax.grad(patch_misfit)(window, illumination, intensity, cosine_table, sine_table)
    return place_patch(summed_total, slope, corner)


def brick_tiles(field):
    components, width_x, width_y, depth_cells = field.shape
    blocks = field.reshape(components, width_x // TILE, TILE, width_y // TILE, TILE, depth_cells)
    blocks = blocks.transpose(1, 3, 0, 2, 4, 5)
    return blocks.reshape(-1, components, TILE * TILE, depth_cells)


def tiles_brick(blocks, width_x, width_y):
    components = blocks.shape[1]
    depth_cells = blocks.shape[3]
    shaped = blocks.reshape(width_x // TILE, width_y // TILE, components, TILE, TILE, depth_cells)
    return shaped.transpose(2, 0, 3, 1, 4, 5).reshape(components, width_x, width_y, depth_cells)


def partial_projection(current, matrices, offsets):
    blocks = brick_tiles(current)
    tile_parts = jnp.einsum("tku,tckz->tcuz", matrices, blocks, preferred_element_type=jnp.float32)
    summed_total = jnp.zeros((2, U, NZ), jnp.float32)
    for tile_index in range(tile_parts.shape[0]):
        anchor = (jnp.zeros((), jnp.int32), offsets[tile_index], jnp.zeros((), jnp.int32))
        before = lax.dynamic_slice(summed_total, anchor, tile_parts.shape[1:])
        summed_total = lax.dynamic_update_slice(
            summed_total, before + tile_parts[tile_index], anchor
        )
    return summed_total


def cut_windows(image, offsets):

    def cut_window(offset):
        anchor = (jnp.zeros((), jnp.int32), offset, jnp.zeros((), jnp.int32))
        return lax.dynamic_slice(image, anchor, (2, TU, NZ))

    return jax.vmap(cut_window)(offsets)


def back_tiles(matrices, windows, width_x, width_y):
    blocks = jnp.einsum("tku,tcuz->tckz", matrices, windows, preferred_element_type=jnp.float32)
    return tiles_brick(blocks, width_x, width_y)


def per_device(
    volume, tile_matrix, tile_offset, patch_count, scan_position, measured, illumination
):
    cosine_table, sine_table = dft_tables(PATCH_SIDE)
    matrices = tile_matrix[0].reshape(-1, TILE * TILE, TU)
    offsets = tile_offset[0].reshape(-1)
    live_count = patch_count[0, 0]
    positions = scan_position[0, 0]
    intensity_values = measured[0, 0]
    width_x = volume.shape[1]
    width_y = volume.shape[2]
    slab_depth = NZ // lax.axis_size("scan")
    slab_start = lax.axis_index("scan") * slab_depth

    def own_slot(slot_index, running, projected_field):
        return patch_term(
            running,
            projected_field,
            positions[slot_index],
            intensity_values[slot_index],
            illumination,
            cosine_table,
            sine_table,
        )

    iterate = lax.dynamic_slice_in_dim(volume, slab_start, slab_depth, 3).astype(jnp.float32)
    projected_field = lax.psum(partial_projection(volume, matrices, offsets), ("vx", "vy"))
    image = lax.psum(
        lax.fori_loop(
            0,
            live_count,
            lambda slot_index, running: own_slot(slot_index, running, projected_field),
            jnp.zeros_like(projected_field),
        ),
        ("vx", "vy"),
    )
    windows = cut_windows(image, offsets).astype(jnp.bfloat16)
    slope = back_tiles(matrices, windows, width_x, width_y)
    slope_sum = lax.psum_scatter(
        slope.astype(jnp.bfloat16), "scan", scatter_dimension=3, tiled=True
    ).astype(jnp.float32)
    iterate = iterate - STEP_LENGTH * slope_sum
    return iterate - lax.dynamic_slice_in_dim(volume, slab_start, slab_depth, 3).astype(jnp.float32)


def solution(mesh):
    in_specs = (
        P(None, "vx", "vy", None),
        P("scan", "vx", "vy", None, None),
        P("scan", "vx", "vy"),
        P("scan", ("vx", "vy")),
        P("scan", ("vx", "vy"), None, None),
        P("scan", ("vx", "vy"), None, None, None),
        P(),
    )
    out_specs = P(None, "vx", "vy", "scan")
    return jax.shard_map(
        per_device, mesh=mesh, in_specs=in_specs, out_specs=out_specs, check_vma=False
    )
```

profile of v0, /device:TPU:0, one launch (start us, length us, event | category | flops | bytes accessed | tf_op | source)
XLA Modules:
  0.0 327.8 jit_solution(10603027786342075903)
XLA Ops:
  6.5 0.0 copy-start
  6.5 0.0 all-reduce.6.cloned.1.call-start
  6.5 1.3 fusion.124
  10.4 1.8 copy.25
  12.2 0.0 copy-done
  12.2 1.0 convolution_bitcast_fusion
  13.2 0.0 copy-start.5
  14.5 0.1 broadcast.46
  14.7 0.0 copy-start.7
  14.7 1.6 dynamic_update_slice.10
  16.3 0.0 copy-start.6
  16.3 0.1 fusion.117
  16.5 1.6 dynamic_update_slice.11
  18.1 0.0 copy-start.3
  18.1 1.0 copy-done.3
  19.1 0.0 all-reduce.6.cloned.1.call-update
  19.1 0.0 reduce-scatter.4.cloned.1.call-start
  19.2 0.0 copy-done.5
  19.2 0.2 copy.27
  19.4 0.0 copy-done.7
  19.4 59.3 %all-reduce.6.cloned.1.call-done = f32[2,512,256]{1,2,0:T(8,128)} async-done(((f32[2,512,256]{1,2,0:T(8,128)}), f32[2,512,256]{1,2,0:T(8,128)}) %all-reduce.6.cloned.1.call-update) | async-done | bytes 1048592 | tf_op jit(solution)/shard_map/psum | solution.py:124
  78.7 1.2 broadcast.46.clone
  79.9 0.0 copy-done.6
  79.9 51.8 %while.12 = (s32[]{:T(128)}, f32[2,512,256]{2,0,1:T(2,128)}, s32[]{:T(128)}, s32[3,2]{0,1:T(2,128)S(1)}, f32[2,512,256]{1,2,0:T(8,128)}, /*index=5*/f32[2,256,25...) while((s32[]{:T(128)}, f32[2,512,256]{2,0,1:T(2,128)}, ...), condition=%wide.region_2.3_spmd.clone.clone, body=%wide.region_1.2_spmd.clone.clone.sunk | while | flops 3240427520 | bytes 30671164 | solution.py:126
  98.5 0.1 constant_dynamic-slice_fusion.4
  98.6 0.5 slice.79
  101.0 2.2 fusion.184
  103.2 1.4 fusion.185
  104.6 1.4 convolution_subtract_fusion.4
  106.0 1.5 fusion.186
  107.4 1.4 fusion.187
  108.8 1.4 convolution_add_fusion.9
  110.2 1.5 convolution_subtract_fusion.5
  111.7 1.5 fusion.188
  113.1 2.4 add_multiply_fusion.3
  115.6 1.4 fusion.191
  117.0 1.4 convolution_add_fusion.11
  118.3 1.4 fusion.189
  119.7 1.4 convolution_add_fusion.10
  121.1 1.5 fusion.190
  122.6 1.5 fusion.192
  124.1 1.5 fusion.193
  125.5 0.0 copy-start.2
  125.5 2.4 fusion.194
  128.0 1.2 fusion.195
  129.2 0.0 copy-done.2
  129.2 0.2 constant_dynamic-slice_fusion.5
  129.4 0.2 copy.43
  129.6 0.1 add_add_fusion.2
  129.7 0.2 copy.44
  129.9 1.0 constant_dynamic-update-slice_fusion.2
  131.7 112.3 %all-reduce.7 = bf16[2,512,256]{2,0,1:T(2,128)(2,1)S(1)} all-reduce(f32[2,512,256]{2,0,1:T(2,128)} %get-tuple-element.94), channel_id=1, replica_groups=mesh['vx'=2,'vy'=4,'scan'=4] {'vx','vy'}, use_global_device_ids=true, to_apply=%region_3.4 | all-reduce | flops 262144 | bytes 1572864 | tf_op jit(solution)/shard_map/psum | solution.py:125
  244.1 1.1 gather_fusion
  245.1 0.8 convert_bitcast_fusion
  245.9 2.6 copy.30
  248.5 1.8 copy.31
  250.3 6.7 %copy.34 = bf16[2,32,64,256]{2,1,0,3:T(8,128)(2,1)} copy(bf16[2,32,64,256]{3,2,1,0:T(8,128)(2,1)S(1)} %bitcast.209) | data formatting | bytes 4194304
  257.0 6.6 %reshape.60 = bf16[256,4096]{1,0:T(8,128)(2,1)} reshape(bf16[256,2,32,64]{3,2,1,0:T(8,128)(2,1)} %bitcast.208) | data formatting | bytes 4194304
  263.6 0.0 reduce-scatter.4.cloned.1.call-update
  263.6 0.0 copy-start.4
  263.6 48.2 %reduce-scatter.4.cloned.1.call-done = bf16[64,4096]{1,0:T(8,128)(2,1)} async-done(((bf16[256,4096]{1,0:T(8,128)(2,1)}), bf16[64,4096]{1,0:T(8,128)(2,1)}) %reduce-scatter.4.cloned.1.call-update) | async-done | bytes 524304
  311.8 2.7 reshape.61
  314.6 2.9 copy.35
  317.5 3.1 subtract_subtract_fusion
  (5 shorter events, 0.0 us)
Async XLA Ops:
  6.5 5.7 %copy-start = (bf16[1,1,2,1024,128]{4,3,2,1,0:T(8,128)(2,1)S(1)}, bf16[1,1,2,1024,128]{4,3,2,1,0:T(8,128)(2,1)}, u32[]{:S(2)}) copy-start(bf16[1,1,2,1024,128]{4,3,2,1,0:T(8,128)(2,1)} %param.10) | copy-start | bytes 1572868
  6.5 72.2 %all-reduce.6.cloned.1.call-start = ((), (), s32[]{:S(2)}) async-start(), calls=%async_computation.1 | async-start | bytes 2097152 | tf_op jit(solution)/shard_map/psum | solution.py:124
  13.2 6.0 %copy-start.5 = (f32[2,256,256]{2,1,0:T(8,128)S(1)}, f32[2,256,256]{2,1,0:T(8,128)}, u32[]{:S(2)}) copy-start(f32[2,256,256]{2,1,0:T(8,128)} %param.15) | copy-start | bytes 1572868
  14.7 4.7 %copy-start.7 = (s32[1,1,2]{2,1,0:T(1,128)S(1)}, s32[1,1,2]{2,1,0:T(1,128)}, u32[]{:S(2)}) copy-start(s32[1,1,2]{2,1,0:T(1,128)} %param.11) | copy-start | bytes 28
  16.3 63.6 %copy-start.6 = (s32[1,1,3,2]{2,3,1,0:T(2,128)S(1)}, s32[1,1,3,2]{2,3,1,0:T(2,128)}, u32[]{:S(2)}) copy-start(s32[1,1,3,2]{2,3,1,0:T(2,128)} %param.13) | copy-start | bytes 76
  18.1 1.0 copy-start.3
  19.1 292.7 %reduce-scatter.4.cloned.1.call-start = ((), (), s32[]{:S(2)}) async-start(), calls=%async_computation.2 | async-start | bytes 2621440
  121.1 4.4 %copy-start.1 = (f32[2,512,256]{1,2,0:T(8,128)S(1)}, f32[2,512,256]{1,2,0:T(8,128)}, u32[]{:S(2)}) copy-start(f32[2,512,256]{1,2,0:T(8,128)} %get-tuple-element.294) | copy-start | bytes 3145732 | tf_op jit(solution)/shard_map/while
  125.5 3.6 %copy-start.2 = (f32[2,512,256]{2,0,1:T(2,128)S(1)}, f32[2,512,256]{2,0,1:T(2,128)}, u32[]{:S(2)}) copy-start(f32[2,512,256]{2,0,1:T(2,128)} %get-tuple-element.279) | copy-start | bytes 3145732 | tf_op jit(solution)/shard_map/while
  263.6 53.9 %copy-start.4 = (bf16[2,32,64,256]{3,2,1,0:T(8,128)(2,1)S(1)}, bf16[2,32,64,256]{3,2,1,0:T(8,128)(2,1)}, u32[]{:S(2)}) copy-start(bf16[2,32,64,256]{3,2,1,0:T(8,128)(2,1)} %param.9) | copy-start | bytes 6291460
Sparse Core Ops, SparseCore 0:
  19.2 59.4 all-reduce.5
  263.7 48.0 reduce-scatter.3
where the time goes:
time: 331 us; the launch traced here: 328 us
  blocking collectives  112 us (34%)
  waiting for transfers between devices  107 us (32%)
  local copies, waits for them, and re-layouts  35.6 us (11%)
  matrix products  26.3 us (8%)
  loops' own time  21.5 us (6%)
  between operations  17.9 us (5%)
  other arithmetic  6.69 us (2%)
    psum x1, blocking collectives, per_device(): lax.psum(lax.fori_loop(0, live_count, lambda slot_index, running: own_slo...  112 us
    psum x1, waiting for transfers between devices, per_device(): lax.psum(partial_projection(volume, matrices, offsets), ('vx', 'vy'))  59.3 us
    unnamed x3, waiting for transfers between devices  48.2 us
    dot_general x16, matrix products, matmul(): return jnp.dot(left, right, precision=lax.Precision.HIGHEST)  24.6 us
    another operation x1, loops' own time, per_device(): lax.fori_loop(0, live_count, lambda slot_index, running: own_slot(slot_in...  21.5 us
    unnamed x17, local copies, waits for them, and re-layouts  20.1 us
  transfers between devices with their start and end apart: 2, of which 2 were waited for; matrix products, arithmetic and copies ran while one was open for 0% of the time, Pallas kernels for 0%

commit v1 on v0

--- a/solution.py
+++ b/solution.py
@@ -122,15 +122,13 @@
 
     iterate = lax.dynamic_slice_in_dim(volume, slab_start, slab_depth, 3).astype(jnp.float32)
     projected_field = lax.psum(partial_projection(volume, matrices, offsets), ("vx", "vy"))
-    image = lax.psum(
-        lax.fori_loop(
-            0,
-            live_count,
-            lambda slot_index, running: own_slot(slot_index, running, projected_field),
-            jnp.zeros_like(projected_field),
-        ),
-        ("vx", "vy"),
+    raw = lax.fori_loop(
+        0,
+        live_count,
+        lambda slot_index, running: own_slot(slot_index, running, projected_field),
+        jnp.zeros_like(projected_field),
     )
+    image = jnp.sum(lax.all_gather(raw, ("vx", "vy")), axis=0)
     windows = cut_windows(image, offsets).astype(jnp.bfloat16)
     slope = back_tiles(matrices, windows, width_x, width_y)
     slope_sum = lax.psum_scatter(

time: 331 us -> 344 us (1.039)
  waiting for transfers between devices: 107 us -> 227 us
  blocking collectives: 112 us -> 0 us
  other arithmetic: 6.69 us -> 10.7 us
    all_gather x0 -> x1, waiting for transfers between devices: none -> 124 us  [per_device(): image = jnp.sum(lax.all_gather(raw, ('vx', 'vy')), axis=0)]
    psum x1 -> x0, blocking collectives: 112 us -> none  [per_device(): lax.psum(lax.fori_loop(0, live_count, lambda slot_index, running: own_slo...]
    unnamed x3 -> x4, waiting for transfers between devices: 48.2 us -> 43.8 us
    reduce_sum x0 -> x1, other arithmetic: none -> 4 us  [per_device(): image = jnp.sum(lax.all_gather(raw, ('vx', 'vy')), axis=0)]
  transfers between devices with their start and end apart: 2 -> 3, of which waited for: 2 -> 3; matrix products, arithmetic and copies ran while one was open for 0% -> 0% of each run, Pallas kernels for 0% -> 0%
where the time goes in v1:
time: 344 us; the launch traced here: 341 us
  waiting for transfers between devices  227 us (66%)
  local copies, waits for them, and re-layouts  38.1 us (11%)
  matrix products  26.3 us (8%)
  loops' own time  21.1 us (6%)
  between operations  17.3 us (5%)
  other arithmetic  10.7 us (3%)
    all_gather x1, waiting for transfers between devices, per_device(): image = jnp.sum(lax.all_gather(raw, ('vx', 'vy')), axis=0)  124 us
    psum x1, waiting for transfers between devices, per_device(): lax.psum(partial_projection(volume, matrices, offsets), ('vx', 'vy'))  59.3 us
    unnamed x4, waiting for transfers between devices  43.8 us
    dot_general x16, matrix products, matmul(): return jnp.dot(left, right, precision=lax.Precision.HIGHEST)  24.6 us
    another operation x1, loops' own time, per_device(): lax.fori_loop(0, live_count, lambda slot_index, running: own_slot(slot_in...  21.1 us
    unnamed x17, local copies, waits for them, and re-layouts  20.2 us
  transfers between devices with their start and end apart: 3, of which 3 were waited for; matrix products, arithmetic and copies ran while one was open for 0% of the time, Pallas kernels for 0%

profile of v1, /device:TPU:0, one launch (start us, length us, event | category | flops | bytes accessed | tf_op | source)
XLA Modules:
  0.0 340.6 jit_solution(14666625585717177067)
XLA Ops:
  6.5 0.0 copy-start
  6.5 1.3 fusion.124
  10.3 1.8 copy.22
  12.1 1.0 convolution_bitcast_fusion
  13.0 0.0 copy-start.5
  14.3 0.1 broadcast.46
  14.5 1.6 dynamic_update_slice.10
  16.1 0.0 copy-start.6
  16.1 0.1 fusion.117
  16.3 1.6 dynamic_update_slice.11
  17.9 0.0 copy-start.3
  17.9 1.0 copy-done.3
  18.9 0.0 all-reduce.5.cloned.1.call-update
  18.9 0.0 all-gather.3.cloned.1.call-start
  18.9 0.0 copy-done.5
  19.0 0.2 copy.24
  19.2 59.3 %all-reduce.5.cloned.1.call-done = f32[2,512,256]{1,2,0:T(8,128)} async-done(((f32[2,512,256]{1,2,0:T(8,128)}), f32[2,512,256]{1,2,0:T(8,128)}) %all-reduce.5.cloned.1.call-update) | async-done | bytes 1048592 | tf_op jit(solution)/shard_map/psum | solution.py:124
  78.5 1.0 broadcast.46.clone
  79.5 53.7 %while.12 = (s32[]{:T(128)}, f32[2,512,256]{2,1,0:T(8,128)}, s32[]{:T(128)}, s32[3,2]{0,1:T(2,128)S(1)}, f32[2,512,256]{1,2,0:T(8,128)}, /*index=5*/f32[2,256,25...) while((s32[]{:T(128)}, f32[2,512,256]{2,1,0:T(8,128)}, ...), condition=%wide.region_2.3_spmd.clone.clone, body=%wide.region_1.2_spmd.clone.clone.sunk | while | flops 3240427520 | bytes 30671164 | solution.py:125
  97.9 0.1 constant_dynamic-slice_fusion.4
  98.0 0.5 slice.79
  100.2 2.2 fusion.184
  102.4 1.4 fusion.185
  103.8 1.4 convolution_subtract_fusion.4
  105.2 1.5 fusion.186
  106.6 1.4 fusion.187
  108.0 1.4 convolution_add_fusion.9
  109.4 1.5 convolution_subtract_fusion.5
  110.9 1.5 fusion.188
  112.3 2.4 add_multiply_fusion.3
  114.8 1.4 fusion.191
  116.2 1.4 convolution_add_fusion.11
  117.5 1.4 fusion.189
  118.9 1.4 convolution_add_fusion.10
  120.3 1.5 fusion.190
  121.8 1.5 fusion.192
  123.2 1.5 fusion.193
  124.7 0.0 copy-start.2
  124.7 2.4 fusion.194
  127.2 1.2 fusion.195
  128.4 0.0 copy-done.2
  128.4 0.1 constant_dynamic-slice_fusion.5
  128.4 0.2 copy.45
  128.6 0.1 add_add_fusion.2
  128.7 0.2 copy.46
  128.9 3.4 %dynamic_update_slice.15 = f32[2,512,256]{2,1,0:T(8,128)} dynamic-update-slice(f32[2,512,256]{2,1,0:T(8,128)} %get-tuple-element.279, f32[2,256,256]{2,1,0:T(8,128)S(1)} %copy.46, s32[]{:T(128)} %constant.22.clone.1..sunk, s32[]{:T(128)S(6)} %select_n.158, s32[]{:T(128)} %constant.22.clone.1..sunk) | dynamic-update-slice | bytes 1048580 | tf_op jit(solution)/shard_map/while/body/dynamic_update_slice | solution.py:45
  133.2 0.0 all-gather.3.cloned.1.call-update
  133.2 0.0 reduce-scatter.4.cloned.1.call-start
  133.3 0.0 copy-done.7
  133.3 123.8 %all-gather.3.cloned.1.call-done = f32[16,512,256]{2,1,0:T(8,128)} async-done(((f32[2,512,256]{2,1,0:T(8,128)}), f32[16,512,256]{2,1,0:T(8,128)}) %all-gather.3.cloned.1.call-update) | async-done | bytes 8388624 | tf_op jit(solution)/shard_map/all_gather | solution.py:131
  257.1 4.0 %reduce_sum.9 = bf16[2,512,256]{2,1,0:T(8,128)(2,1)S(1)} reduce(f32[8,2,512,256]{3,2,1,0:T(8,128)} %bitcast.211, f32[]{:T(128)} %constant.26.clone.1), dimensions={0}, to_apply=%region_3.4 | reduce | flops 1835008 | bytes 8912900 | tf_op jit(solution)/shard_map/reduce_sum | solution.py:131
  261.1 0.5 copy.27
  261.6 1.1 gather_fusion
  262.7 0.8 convert_bitcast_fusion
  263.4 2.6 copy.29
  266.0 1.8 copy.30
  267.8 6.7 %copy.33 = bf16[2,32,64,256]{2,1,0,3:T(8,128)(2,1)} copy(bf16[2,32,64,256]{3,2,1,0:T(8,128)(2,1)S(1)} %bitcast.210) | data formatting | bytes 4194304
  274.5 6.6 %reshape.61 = bf16[256,4096]{1,0:T(8,128)(2,1)} reshape(bf16[256,2,32,64]{3,2,1,0:T(8,128)(2,1)} %bitcast.209) | data formatting | bytes 4194304
  281.1 0.0 reduce-scatter.4.cloned.1.call-update
  281.2 0.0 copy-start.4
  281.2 43.8 %reduce-scatter.4.cloned.1.call-done = bf16[64,4096]{1,0:T(8,128)(2,1)} async-done(((bf16[256,4096]{1,0:T(8,128)(2,1)}), bf16[64,4096]{1,0:T(8,128)(2,1)}) %reduce-scatter.4.cloned.1.call-update) | async-done | bytes 524304
  324.9 2.7 reshape.62
  327.7 2.9 copy.34
  330.6 3.1 subtract_subtract_fusion
  (9 shorter events, 0.0 us)
Async XLA Ops:
  6.5 5.5 %copy-start = (bf16[1,1,2,1024,128]{4,3,2,1,0:T(8,128)(2,1)S(1)}, bf16[1,1,2,1024,128]{4,3,2,1,0:T(8,128)(2,1)}, u32[]{:S(2)}) copy-start(bf16[1,1,2,1024,128]{4,3,2,1,0:T(8,128)(2,1)} %param.10) | copy-start | bytes 1572868
  6.5 71.9 %all-reduce.5.cloned.1.call-start = ((), (), s32[]{:S(2)}) async-start(), calls=%async_computation.1 | async-start | bytes 2097152 | tf_op jit(solution)/shard_map/psum | solution.py:124
  13.0 5.9 %copy-start.5 = (f32[2,256,256]{2,1,0:T(8,128)S(1)}, f32[2,256,256]{2,1,0:T(8,128)}, u32[]{:S(2)}) copy-start(f32[2,256,256]{2,1,0:T(8,128)} %param.15) | copy-start | bytes 1572868
  16.1 63.4 %copy-start.6 = (s32[1,1,3,2]{2,3,1,0:T(2,128)S(1)}, s32[1,1,3,2]{2,3,1,0:T(2,128)}, u32[]{:S(2)}) copy-start(s32[1,1,3,2]{2,3,1,0:T(2,128)} %param.13) | copy-start | bytes 76
  17.9 1.0 copy-start.3
  18.9 238.2 %all-gather.3.cloned.1.call-start = ((), (), s32[]{:S(2)}) async-start(), calls=%async_computation.2 | async-start | bytes 9437184 | tf_op jit(solution)/shard_map/all_gather | solution.py:131
  79.5 53.8 %copy-start.7 = (s32[1,1,2]{2,1,0:T(1,128)S(1)}, s32[1,1,2]{2,1,0:T(1,128)}, u32[]{:S(2)}) copy-start(s32[1,1,2]{2,1,0:T(1,128)} %param.11) | copy-start | bytes 28
  120.3 4.4 %copy-start.1 = (f32[2,512,256]{1,2,0:T(8,128)S(1)}, f32[2,512,256]{1,2,0:T(8,128)}, u32[]{:S(2)}) copy-start(f32[2,512,256]{1,2,0:T(8,128)} %get-tuple-element.294) | copy-start | bytes 3145732 | tf_op jit(solution)/shard_map/while
  124.7 3.6 %copy-start.2 = (f32[2,512,256]{2,1,0:T(8,128)S(1)}, f32[2,512,256]{2,1,0:T(8,128)}, u32[]{:S(2)}) copy-start(f32[2,512,256]{2,1,0:T(8,128)} %get-tuple-element.279) | copy-start | bytes 3145732 | tf_op jit(solution)/shard_map/while
  133.2 191.7 %reduce-scatter.4.cloned.1.call-start = ((), (), s32[]{:S(2)}) async-start(), calls=%async_computation.3 | async-start | bytes 2621440
  281.2 49.5 %copy-start.4 = (bf16[2,32,64,256]{3,2,1,0:T(8,128)(2,1)S(1)}, bf16[2,32,64,256]{3,2,1,0:T(8,128)(2,1)}, u32[]{:S(2)}) copy-start(bf16[2,32,64,256]{3,2,1,0:T(8,128)(2,1)} %param.9) | copy-start | bytes 6291460
Sparse Core Ops, SparseCore 0:
  19.0 59.4 all-reduce.4
  133.3 123.6 all-gather.2
  281.3 43.6 reduce-scatter.3
